TPU v7x, 128 devices: a whole 4x4x4 slice. The times are simulated.
128 devices in a mesh: dp: 16 (over z, y), expert: 8 (over x, core).
Axes of the slice: x: 4, y: 4, z: 4, core: 2. Of those that a mesh axis runs over, the one named last changes fastest.
Arguments:
- hidden: bfloat16 [8, 1024, 8192], P('expert', None, 'dp'), may hold values from -6 to 6
- down_weight: bfloat16 [8, 8192, 6144], P('expert', 'dp'), may hold values from -0.0625 to 0.0625
- grad_out: bfloat16 [2048, 6144], P('dp', 'expert'), may hold values from -2 to 2
- routing: int32 [2048, 2], P('dp'), may hold values from 0 to 7, all different within a row; in each aligned block of 128 rows (0 to 127, 128 to 255, ...) at most 64 rows name the same one
- gates: float32 [2048, 2], P('dp'), may hold values from 0.25 to 1
Outputs:
- mixed_out: bfloat16 [2048, 6144], P('dp', 'expert')
- grad_hidden: bfloat16 [8, 1024, 8192], P('expert', None, 'dp')
- grad_weight: bfloat16 [8, 8192, 6144], P('expert', 'dp')
Inputs may be any that keep to these rules, and one draw needn't show every extreme that they name: `routing`: among the 128 tokens of one sequence shard (aligned blocks of rows), each expert is named by at most 64 tokens, a bound that some block reaches; a token names 2 different experts.
All inputs are finite; a program needn't handle non-finite values.
Results may differ from a plain program's by a relative error of at most 0.017.
Values may be sent and summed in bfloat16 or wider, within the bound.
A program may use at most 128 MiB of HBM per device.

v0:
```python
import jax
import jax.numpy as jnp
from jax import lax
from jax.sharding import PartitionSpec as P


def dispatch_weights(routing, gates, experts, capacity):
    flattened = routing.reshape(-1)
    onehot = (flattened[:, None] == jnp.arange(experts, dtype=jnp.int32)[None, :]).astype(jnp.int32)
    position = jnp.sum((jnp.cumsum(onehot, axis=0) - onehot) * onehot, axis=1)
    target = flattened * capacity + position
    picked = (jnp.arange(experts * capacity, dtype=jnp.int32)[:, None] == target[None, :]).astype(
        jnp.float32
    )
    picked = picked * gates.reshape(-1)[None, :]
    return jnp.sum(picked.reshape(experts * capacity, routing.shape[0], routing.shape[1]), axis=2)


def body(hidden, down_weight, grad_out, routing, gates):
    highest = lax.Precision.HIGHEST
    groups = lax.axis_size("dp")
    owners = lax.axis_size("expert")
    experts = hidden.shape[0] * owners
    slot_total = hidden.shape[1]
    capacity = slot_total // groups
    dispatch = dispatch_weights(routing, gates, experts, capacity)
    hidden_rows = hidden[0]
    weight = down_weight[0]
    own_rows = lax.psum_scatter(
        jnp.dot(hidden_rows, weight, preferred_element_type=jnp.float32).astype(jnp.bfloat16),
        "dp",
        scatter_dimension=0,
        tiled=True,
    ).astype(jnp.float32)
    own_rows = own_rows.astype(jnp.bfloat16)[None]
    outputs = lax.all_to_all(own_rows, "expert", split_axis=2, concat_axis=0, tiled=True)
    flat_outputs = outputs.reshape(experts * capacity, outputs.shape[-1]).astype(jnp.float32)
    mixed_out = lax.dot_general(dispatch, flat_outputs, (((0,), (0,)), ((), ())), precision=highest)
    mixed_out = mixed_out.astype(jnp.bfloat16)
    routed = jnp.dot(dispatch, grad_out.astype(jnp.float32), precision=highest).astype(jnp.bfloat16)
    routed = routed.reshape(experts, capacity, routed.shape[-1])
    shards = lax.all_gather(routed, "dp", axis=1, tiled=True)
    gathered = lax.all_to_all(shards, "expert", split_axis=0, concat_axis=2, tiled=True)
    grad_rows = gathered[0]
    hidden_acc = lax.dot_general(
        grad_rows, weight, (((1,), (1,)), ((), ())), preferred_element_type=jnp.float32
    )
    weight_acc = lax.dot_general(
        hidden_rows, grad_rows, (((0,), (0,)), ((), ())), preferred_element_type=jnp.float32
    )
    grad_hidden = hidden_acc.astype(jnp.bfloat16)[None]
    grad_weight = weight_acc.astype(jnp.bfloat16)[None]
    return (mixed_out, grad_hidden, grad_weight)


def solution(mesh):
    return jax.shard_map(
        body,
        mesh=mesh,
        in_specs=(
            P("expert", None, "dp"),
            P("expert", "dp", None),
            P("dp", "expert"),
            P("dp", None),
            P("dp", None),
        ),
        out_specs=(P("dp", "expert"), P("expert", None, "dp"), P("expert", "dp", None)),
        check_vma=False,
    )
```

profile of v0, /device:TPU:1, one launch (start us, length us, event | category | flops | bytes accessed | tf_op | source)
XLA Modules:
  0.0 412.6 jit_solution(2753633807053152809)
XLA Ops:
  7.2 1.2 copy-done
  8.4 12.3 %convolution_convert_fusion = bf16[1024,6144]{1,0:T(8,128)(2,1)} fusion(bf16[1,512,6144]{2,1,0:T(8,128)(2,1)} %param.6, bf16[1,1024,512]{2,1,0:T(8,128)(2,1)S(1)} %copy-done), kind=kOutput, calls=%fused_computation | convolution fusion | flops 6448742400 | bytes 19922944 | tf_op jit(solution)/shard_map/dot_general | solution.py:30
  20.7 0.6 copy-done.2
  21.3 0.1 copy.50
  21.5 0.1 eq.44
  21.6 0.1 eq.40
  21.8 0.6 reduce-window.6
  22.3 0.2 slice_reduce_fusion
  22.6 0.1 fusion.13
  22.7 0.1 reduce_sum.21
  22.8 0.1 copy.52
  22.9 0.1 select_reduce_fusion
  23.0 0.8 convolution_convert_fusion.2
  23.8 1.3 copy.56
  25.1 93.8 %reduce-scatter.2.cloned.1.call-done = bf16[64,6144]{1,0:T(8,128)(2,1)} async-done(((bf16[1024,6144]{1,0:T(8,128)(2,1)}), bf16[64,6144]{1,0:T(8,128)(2,1)}) %reduce-scatter.2.cloned.1.call-update) | async-done | bytes 786448 | tf_op jit(solution)/shard_map/reduce_scatter | solution.py:29
  118.9 7.2 %copy.53 = bf16[1,64,6144]{1,0,2:T(2,128)(2,1)} copy(bf16[1,64,6144]{2,1,0:T(8,128)(2,1)} %bitcast.58) | data formatting | bytes 1572864 | tf_op jit(solution)/shard_map/broadcast_in_dim | solution.py:35
  126.1 0.5 broadcast.37
  126.6 34.3 %reduce.2 = bf16[6144,64]{1,0:T(8,128)(2,1)S(1)} reduce(bf16[6144,1,64]{2,1,0:T(2,128)(2,1)} %bitcast.52, bf16[]{:T(256)} %broadcast.37), dimensions={1}, to_apply=%bitcast.43.reduce_sub_computation | reduce | bytes 1572866
  161.0 1.9 reshape.59
  162.9 5.4 %all-to-all-start = ((bf16[8,2,24576]{2,1,0:T(2,128)(2,1)}), bf16[8,2,24576]{2,1,0:T(2,128)(2,1)S(1)}, u32[]{:S(2)}, u32[]{:S(2)}) async-start(bf16[8,2,24576]{2,1,0:T(2,128)(2,1)} %reshape.59), calls=%async_computation.1 | async-start | bytes 1572864 | tf_op jit(solution)/shard_map/all_to_all | solution.py:36
  168.3 41.9 %all-gather.2.cloned.1.call-done = bf16[8,1024,768]{2,0,1:T(8,128)(2,1)} async-done(((bf16[8,64,768]{2,0,1:T(8,128)(2,1)}), bf16[8,1024,768]{2,0,1:T(8,128)(2,1)}) %all-gather.2.cloned.1.call-update) | async-done | bytes 12582928 | tf_op jit(solution)/shard_map/all_gather | solution.py:42
  210.2 16.5 %copy.57 = bf16[8,1024,768]{1,2,0:T(8,128)(2,1)} copy(bf16[8,1024,768]{2,0,1:T(8,128)(2,1)} %all-gather.2.cloned.1.call-done) | data formatting | bytes 25165824 | tf_op jit(solution)/shard_map/all_gather | solution.py:42
  226.7 6.2 %all-to-all-start.1 = ((bf16[8,1024,768]{1,2,0:T(8,128)(2,1)}), bf16[8,1024,768]{1,2,0:T(8,128)(2,1)}, u32[]{:S(2)}, u32[]{:S(2)}) async-start(bf16[8,1024,768]{1,2,0:T(8,128)(2,1)} %copy.57), calls=%async_computation.2 | async-start | bytes 25165824 | tf_op jit(solution)/shard_map/all_to_all | solution.py:43
  232.9 3.9 reshape.60
  236.9 6.0 %copy.54 = bf16[1,64,6144]{2,1,0:T(8,128)(2,1)S(1)} copy(bf16[1,64,6144]{1,0,2:T(2,128)(2,1)} %bitcast.53) | data formatting | bytes 1572864 | tf_op jit(solution)/shard_map/all_to_all | solution.py:36
  242.9 0.1 copy.59
  243.1 0.1 copy.55
  243.3 1.2 convolution_convert_fusion.3
  244.5 127.1 %all-to-all-done.1 = bf16[8,1024,768]{1,2,0:T(8,128)(2,1)} async-done(((bf16[8,1024,768]{1,2,0:T(8,128)(2,1)}), bf16[8,1024,768]{1,2,0:T(8,128)(2,1)}, u32[]{:S(2)}, u32[]{:S(2)}) %all-to-all-start.1) | async-done | bytes 12582944 | tf_op jit(solution)/shard_map/all_to_all | solution.py:43
  371.6 12.4 %fusion.7 = bf16[1,1024,512]{2,1,0:T(8,128)(2,1)} fusion(bf16[1024,6144]{0,1:T(8,128)(2,1)} %bitcast.10, bf16[1,512,6144]{2,1,0:T(8,128)(2,1)} %param.6), kind=kOutput, calls=%fused_computation.8 | convolution fusion | flops 6442975232 | bytes 19922944 | tf_op jit(solution)/shard_map/dot_general | solution.py:45
  384.0 13.1 %fusion = bf16[1,512,6144]{1,2,0:T(8,128)(2,1)} fusion(bf16[1024,6144]{0,1:T(8,128)(2,1)} %bitcast.10, bf16[1,1024,512]{2,1,0:T(8,128)(2,1)S(1)} %copy-done), kind=kOutput, calls=%fused_computation.2 | convolution fusion | flops 6445596672 | bytes 19922944 | tf_op jit(solution)/shard_map/dot_general | solution.py:48
  397.2 8.6 %copy.58 = bf16[1,512,6144]{2,1,0:T(8,128)(2,1)} copy(bf16[1,512,6144]{1,2,0:T(8,128)(2,1)} %fusion) | data formatting | bytes 12582912
  (16 shorter events, 0.2 us)
Async XLA Ops:
  7.2 1.2 copy-start
  7.2 111.7 %reduce-scatter.2.cloned.1.call-start = ((), (), s32[]{:S(2)}) async-start(), calls=%async_computation.3 | async-start | bytes 13369344 | tf_op jit(solution)/shard_map/reduce_scatter | solution.py:29
  20.7 0.7 copy-start.2
  20.7 2.2 copy-start.3
  20.7 2.3 copy-start.1
  20.7 189.5 %all-gather.2.cloned.1.call-start = ((), (), s32[]{:S(2)}) async-start(), calls=%async_computation.4 | async-start | bytes 13369344 | tf_op jit(solution)/shard_map/all_gather | solution.py:42
  162.9 63.8 %all-to-all-start = ((bf16[8,2,24576]{2,1,0:T(2,128)(2,1)}), bf16[8,2,24576]{2,1,0:T(2,128)(2,1)S(1)}, u32[]{:S(2)}, u32[]{:S(2)}) async-start(bf16[8,2,24576]{2,1,0:T(2,128)(2,1)} %reshape.59), calls=%async_computation.1 | async-start | bytes 1572864 | tf_op jit(solution)/shard_map/all_to_all | solution.py:36
  226.7 144.9 %all-to-all-start.1 = ((bf16[8,1024,768]{1,2,0:T(8,128)(2,1)}), bf16[8,1024,768]{1,2,0:T(8,128)(2,1)}, u32[]{:S(2)}, u32[]{:S(2)}) async-start(bf16[8,1024,768]{1,2,0:T(8,128)(2,1)} %copy.57), calls=%async_computation.2 | async-start | bytes 25165824 | tf_op jit(solution)/shard_map/all_to_all | solution.py:43
Sparse Core Ops, SparseCore 0:
  20.8 98.0 reduce-scatter.1
  121.0 89.1 all-gather.1
where the time goes:
time: 414 us; the launch traced here: 413 us
  waiting for transfers between devices  263 us (64%)
  local copies, waits for them, and re-layouts  49 us (12%)
  matrix products  39.8 us (10%)
  other arithmetic  35.1 us (8%)
  between operations  14.1 us (3%)
  starting transfers between devices  11.7 us (3%)
    all_to_all x1, waiting for transfers between devices, body(): lax.all_to_all(shards, 'expert', split_axis=0, concat_axis=2, tiled=True)  127 us
    reduce_scatter x1, waiting for transfers between devices, body(): lax.psum_scatter(jnp.dot(hidden_rows, weight, preferred_element_type=jnp....  93.8 us
    all_gather x1, waiting for transfers between devices, body(): shards = lax.all_gather(routed, 'dp', axis=1, tiled=True)  41.9 us
    unnamed x1, other arithmetic  34.3 us
    unnamed x14, local copies, waits for them, and re-layouts  17 us
    all_gather x1, local copies, waits for them, and re-layouts, body(): shards = lax.all_gather(routed, 'dp', axis=1, tiled=True)  16.5 us
    dot_general x1, matrix products, body(): lax.dot_general(hidden_rows, grad_rows, (((0,), (0,)), ((), ())), preferr...  13.1 us
    dot_general x1, matrix products, body(): lax.dot_general(grad_rows, weight, (((1,), (1,)), ((), ())), preferred_el...  12.4 us
  transfers between devices with their start and end apart: 4, of which 3 were waited for; matrix products, arithmetic and copies ran while one was open for 18% of the time, Pallas kernels for 0%

commit v1 on v0

--- a/solution.py
+++ b/solution.py
@@ -39,7 +39,8 @@
     mixed_out = mixed_out.astype(jnp.bfloat16)
     routed = jnp.dot(dispatch, grad_out.astype(jnp.float32), precision=highest).astype(jnp.bfloat16)
     routed = routed.reshape(experts, capacity, routed.shape[-1])
-    shards = lax.all_gather(routed, "dp", axis=1, tiled=True)
+    mid_arr = jnp.stack([routed for _ in range(lax.axis_size("dp"))])
+    shards = jnp.concatenate(lax.all_to_all(mid_arr, "dp", 0, 0), axis=1)
     gathered = lax.all_to_all(shards, "expert", split_axis=0, concat_axis=2, tiled=True)
     grad_rows = gathered[0]
     hidden_acc = lax.dot_general(

time: 414 us -> 481 us (1.16)
  blocking collectives: 0 us -> 330 us
  waiting for transfers between devices: 263 us -> 0.02 us
  starting transfers between devices: 11.7 us -> 4.72 us
  local copies, waits for them, and re-layouts: 49 us -> 55.9 us
    all_to_all x0 -> x2, blocking collectives: none -> 330 us  [the longest x1 185 us: body(): shards = jnp.concatenate(lax.all_to_all(mid_arr, 'dp', 0, 0), axis=1)]
    all_to_all x1 -> x0, waiting for transfers between devices: 127 us -> none  [body(): lax.all_to_all(shards, 'expert', split_axis=0, concat_axis=2, tiled=True)]
    reduce_scatter x1, waiting for transfers between devices: 93.8 us -> 0.01 us  [body(): lax.psum_scatter(jnp.dot(hidden_rows, weight, preferred_element_type=jnp....]
    all_gather x1 -> x0, waiting for transfers between devices: 41.9 us -> none  [body(): shards = lax.all_gather(routed, 'dp', axis=1, tiled=True)]
    all_to_all x0 -> x2, local copies, waits for them, and re-layouts: none -> 18.6 us  [the longest x1 16.6 us: body(): lax.all_to_all(shards, 'expert', split_axis=0, concat_axis=2, tiled=True)]
    all_gather x1 -> x0, local copies, waits for them, and re-layouts: 16.5 us -> none  [body(): shards = lax.all_gather(routed, 'dp', axis=1, tiled=True)]
    all_to_all x1 -> x0, starting transfers between devices: 6.24 us -> none  [body(): lax.all_to_all(shards, 'expert', split_axis=0, concat_axis=2, tiled=True)]
    another operation x1 -> x2, local copies, waits for them, and re-layouts: 0.01 us -> 6.05 us  [the longest x1 6.05 us: body(): mid_arr = jnp.stack([routed for _ in range(lax.axis_size('dp'))])]
  transfers between devices with their start and end apart: 4 -> 2, of which waited for: 3 -> 0; matrix products, arithmetic and copies ran while one was open for 18% -> 13% of each run, Pallas kernels for 0% -> 0%
where the time goes in v1:
time: 481 us; the launch traced here: 479 us
  blocking collectives  330 us (69%)
  local copies, waits for them, and re-layouts  55.9 us (12%)
  matrix products  39.9 us (8%)
  other arithmetic  35.1 us (7%)
  between operations  14.1 us (3%)
    all_to_all x1, blocking collectives, body(): shards = jnp.concatenate(lax.all_to_all(mid_arr, 'dp', 0, 0), axis=1)  185 us
    all_to_all x1, blocking collectives, body(): lax.all_to_all(shards, 'expert', split_axis=0, concat_axis=2, tiled=True)  145 us
    unnamed x1, other arithmetic  34.3 us
    unnamed x16, local copies, waits for them, and re-layouts  17.1 us
    all_to_all x1, local copies, waits for them, and re-layouts, body(): lax.all_to_all(shards, 'expert', split_axis=0, concat_axis=2, tiled=True)  16.6 us
    dot_general x1, matrix products, body(): lax.dot_general(hidden_rows, grad_rows, (((0,), (0,)), ((), ())), preferr...  13.2 us
    dot_general x1, matrix products, body(): lax.dot_general(grad_rows, weight, (((1,), (1,)), ((), ())), preferred_el...  12.4 us
    dot_general x1, matrix products, body(): jnp.dot(hidden_rows, weight, preferred_element_type=jnp.float32)  12.3 us
  transfers between devices with their start and end apart: 2, of which 0 were waited for; matrix products, arithmetic and copies ran while one was open for 13% of the time, Pallas kernels for 0%

profile of v1, /device:TPU:1, one launch (start us, length us, event | category | flops | bytes accessed | tf_op | source)
XLA Modules:
  0.0 479.4 jit_solution(1901993128615095233)
XLA Ops:
  7.2 1.2 copy-done
  8.4 12.3 %convolution_convert_fusion = bf16[1024,6144]{1,0:T(8,128)(2,1)} fusion(bf16[1,512,6144]{2,1,0:T(8,128)(2,1)} %param.6, bf16[1,1024,512]{2,1,0:T(8,128)(2,1)S(1)} %copy-done), kind=kOutput, calls=%fused_computation | convolution fusion | flops 6448742400 | bytes 19922944 | tf_op jit(solution)/shard_map/dot_general | solution.py:30
  20.8 0.6 copy-done.3
  21.4 0.1 copy.50
  21.5 0.1 eq.44
  21.7 0.6 reduce-window.6
  22.3 0.2 slice_reduce_fusion
  22.5 0.1 eq.40
  22.7 0.1 fusion.13
  22.8 0.1 reduce_sum.21
  22.9 0.1 copy.52
  23.0 0.1 select_reduce_fusion
  23.1 0.8 convolution_convert_fusion.2
  23.8 6.0 %stack.3 = bf16[16,8,64,768]{3,2,1,0:T(8,128)(2,1)} broadcast(bf16[8,64,768]{2,1,0:T(8,128)(2,1)S(1)} %bitcast.60), dimensions={1,2,3} | broadcast | bytes 13369344 | tf_op jit(solution)/shard_map/stack | solution.py:42
  29.9 184.8 %all_to_all.35 = bf16[16,8,64,768]{3,2,1,0:T(8,128)(2,1)S(1)} all-to-all(bf16[16,8,64,768]{3,2,1,0:T(8,128)(2,1)} %stack.3), channel_id=1, replica_groups=mesh['dp'=16,'expert'=8] {'dp'}, dimensions={0} | all-to-all | bytes 25165824 | tf_op jit(solution)/shard_map/all_to_all | solution.py:43
  214.7 1.9 copy.56
  216.6 144.8 %all_to_all.36 = bf16[8,1024,768]{2,1,0:T(8,128)(2,1)} all-to-all(bf16[8,1024,768]{2,1,0:T(8,128)(2,1)S(1)} %bitcast.54), channel_id=1, replica_groups=mesh['dp'=16,'expert'=8] {'expert'}, dimensions={0} | all-to-all | bytes 25165824 | tf_op jit(solution)/shard_map/all_to_all | solution.py:44
  361.4 16.6 %copy.57 = bf16[1,1024,8,768]{1,3,2,0:T(8,128)(2,1)} copy(bf16[1,1024,8,768]{3,1,2,0:T(8,128)(2,1)} %bitcast.55) | data formatting | bytes 25165824 | tf_op jit(solution)/shard_map/all_to_all | solution.py:44
  378.0 13.2 %fusion = bf16[1,512,6144]{1,2,0:T(8,128)(2,1)} fusion(bf16[1024,6144]{0,1:T(8,128)(2,1)} %bitcast.56, bf16[1,1024,512]{2,1,0:T(8,128)(2,1)S(1)} %copy-done), kind=kOutput, calls=%fused_computation.2 | convolution fusion | flops 6445596672 | bytes 19922944 | tf_op jit(solution)/shard_map/dot_general | solution.py:49
  391.2 7.2 %copy.53 = bf16[1,64,6144]{1,0,2:T(2,128)(2,1)} copy(bf16[1,64,6144]{2,1,0:T(8,128)(2,1)} %bitcast.64) | data formatting | bytes 1572864 | tf_op jit(solution)/shard_map/broadcast_in_dim | solution.py:35
  398.5 0.5 broadcast.38
  399.0 34.3 %reduce.2 = bf16[6144,64]{1,0:T(8,128)(2,1)S(1)} reduce(bf16[6144,1,64]{2,1,0:T(2,128)(2,1)} %bitcast.58, bf16[]{:T(256)} %broadcast.38), dimensions={1}, to_apply=%bitcast.45.reduce_sub_computation | reduce | bytes 1572866
  433.3 1.9 reshape.65
  435.2 4.7 all-to-all-start
  439.9 12.4 %fusion.7 = bf16[1,1024,512]{2,1,0:T(8,128)(2,1)} fusion(bf16[1024,6144]{0,1:T(8,128)(2,1)} %bitcast.57, bf16[1,512,6144]{2,1,0:T(8,128)(2,1)} %param.6), kind=kOutput, calls=%fused_computation.8 | convolution fusion | flops 6442975232 | bytes 19922944 | tf_op jit(solution)/shard_map/dot_general | solution.py:46
  452.3 8.6 %copy.58 = bf16[1,512,6144]{2,1,0:T(8,128)(2,1)} copy(bf16[1,512,6144]{1,2,0:T(8,128)(2,1)} %fusion) | data formatting | bytes 12582912
  460.9 4.0 reshape.66
  464.9 6.0 %copy.54 = bf16[1,64,6144]{2,1,0:T(8,128)(2,1)S(1)} copy(bf16[1,64,6144]{1,0,2:T(2,128)(2,1)} %bitcast.59) | data formatting | bytes 1572864 | tf_op jit(solution)/shard_map/all_to_all | solution.py:36
  471.0 0.1 copy.59
  471.2 0.1 bitcast_bitcast_fusion
  471.2 0.1 copy.55
  471.4 1.2 convolution_convert_fusion.3
  (16 shorter events, 0.1 us)
Async XLA Ops:
  7.2 1.2 copy-start
  7.2 384.0 %reduce-scatter.2.cloned.1.call-start = ((), (), s32[]{:S(2)}) async-start(), calls=%async_computation.4 | async-start | bytes 13369344 | tf_op jit(solution)/shard_map/reduce_scatter | solution.py:29
  20.7 0.7 copy-start.3
  20.7 2.2 copy-start.4
  20.7 2.3 copy-start.2
  435.2 25.7 %all-to-all-start = ((bf16[8,2,24576]{2,1,0:T(2,128)(2,1)}), bf16[8,2,24576]{2,1,0:T(2,128)(2,1)S(1)}, u32[]{:S(2)}, u32[]{:S(2)}) async-start(bf16[8,2,24576]{2,1,0:T(2,128)(2,1)} %reshape.65), calls=%async_computation.1 | async-start | bytes 1572864 | tf_op jit(solution)/shard_map/all_to_all | solution.py:36
  439.9 32.7 %copy-start.1 = (bf16[1,1024,512]{2,1,0:T(8,128)(2,1)S(1)}, bf16[1,1024,512]{2,1,0:T(8,128)(2,1)}, u32[]{:S(2)}) copy-start(bf16[1,1024,512]{2,1,0:T(8,128)(2,1)} %param.5) | copy-start | bytes 3145732
Sparse Core Ops, SparseCore 0:
  20.9 229.3 reduce-scatter.1
